TPU v7x, 256 devices: a whole 4x4x8 slice. The times are simulated.
256 devices in a mesh: row: 16 (over y, z_lo, core), col: 16 (over x, z_hi).
Axes of the slice: x: 4, y: 4, z: 8 (z_hi: 4, z_lo: 2; z = z_hi * 2 + z_lo), core: 2. Of those that a mesh axis runs over, the one named last changes fastest.
Arguments:
- points: float32 [32, 24576], P(None, ('row', 'col')), may hold values from -6 to 6
- targets: float32 [24576], P(('row', 'col')), may hold values from -6 to 6
- probes: float32 [8, 24576], P(None, ('row', 'col')), may hold values from -6 to 6
- lengthscale: float32 [4], replicated, may hold values from 2.4 to 3.4
- outputscale: float32 [4], replicated, may hold values from 0.5 to 2
- noise_var: float32 [4], replicated, may hold values from 0.1 to 1
Outputs:
- solution: float32 [12, 24576], P(None, ('row', 'col'))
- residual: float32 [12, 24576], P(None, ('row', 'col'))
All inputs are finite; a program needn't handle non-finite values.
Results may differ from a plain program's by a relative error of at most 0.009.
Values may be sent and summed in bfloat16 or wider, within the bound.
A program may use at most 64 MiB of HBM per device.

v0:
```python
import math
import jax
import jax.numpy as jnp
from jax import lax
from jax.sharding import PartitionSpec as P

ITERATIONS = 2


def sq_distance(rows_x, cols_x):
    inner_prod = lax.dot_general(
        rows_x,
        cols_x,
        (((0,), (0,)), ((), ())),
        precision=lax.Precision.HIGHEST,
        preferred_element_type=jnp.float32,
    )
    sq_rows = jnp.sum(rows_x * rows_x, axis=0)
    sq_cols = jnp.sum(cols_x * cols_x, axis=0)
    return sq_rows[:, None] + sq_cols[None, :] - 2.0 * inner_prod


def make_tiles(distance, negscale, outputscale):
    return [
        (outputscale[p] * jnp.exp(distance * negscale[p])).astype(jnp.bfloat16)
        for p in range(negscale.shape[0])
    ]


def apply_tiles(tiles, dir_cols, width):
    products = []
    for p in range(len(tiles)):
        products.append(
            lax.dot_general(
                dir_cols[p * width : (p + 1) * width],
                tiles[p],
                (((1,), (1,)), ((), ())),
                preferred_element_type=jnp.float32,
            )
        )
    return jnp.concatenate(products, axis=0)


def on_device(points, targets, probes, lengthscale, outputscale, noise_var):
    n_part = lengthscale.shape[0]
    width = probes.shape[0] // n_part + 1
    right_side = jnp.concatenate(
        [
            jnp.concatenate(
                [targets[None, :], probes[p * (width - 1) : (p + 1) * (width - 1)]], axis=0
            )
            for p in range(n_part)
        ],
        axis=0,
    )
    negscale = -0.5 / (lengthscale * lengthscale)
    noisevec = jnp.repeat(noise_var, width)[:, None]
    rows_x = lax.all_gather(points, "col", axis=1, tiled=True)
    cols_x = lax.all_gather(points, "row", axis=1, tiled=True)
    row_count = rows_x.shape[1]
    row_block = math.gcd(row_count, 512)
    n_blocks = row_count // row_block
    kept = [
        make_tiles(
            sq_distance(rows_x[:, k * row_block : (k + 1) * row_block], cols_x),
            negscale,
            outputscale,
        )
        for k in range(n_blocks)
    ]
    solution = jnp.zeros_like(right_side)
    residual = right_side
    direction = right_side
    res_norm = lax.psum(jnp.sum(residual * residual, axis=1), ("row", "col"))
    for iteration in range(ITERATIONS):
        dir_cols = lax.all_gather(direction.astype(jnp.bfloat16), "row", axis=1, tiled=True)
        pieces = []
        for apply_k in range(n_blocks):
            tiles = kept[apply_k]
            pieces.append(apply_tiles(tiles, dir_cols, width))
        partial_value = jnp.concatenate(pieces, axis=1)
        applied = (
            lax.psum_scatter(partial_value, "col", scatter_dimension=1, tiled=True)
            + noisevec * direction
        )
        curvature = lax.psum(jnp.sum(direction * applied, axis=1), ("row", "col"))
        applied, curvature = (applied, curvature)
        step_size = (res_norm / curvature)[:, None]
        solution = solution + step_size * direction
        residual = residual - step_size * applied
        if iteration + 1 < ITERATIONS:
            fresh_norm = lax.psum(jnp.sum(residual * residual, axis=1), ("row", "col"))
            direction = residual + (fresh_norm / res_norm)[:, None] * direction
            res_norm = fresh_norm
    return (solution, residual)


def solution(mesh):
    placed = (P(None, ("row", "col")), P(("row", "col")), P(None, ("row", "col")), P(), P(), P())
    return jax.shard_map(
        on_device,
        mesh=mesh,
        in_specs=placed,
        out_specs=(P(None, ("row", "col")), P(None, ("row", "col"))),
        check_vma=False,
    )
```

profile of v0, /device:TPU:1, one launch (start us, length us, event | category | flops | bytes accessed | tf_op | source)
XLA Modules:
  0.0 570.3 jit_solution(6471585392873921023)
XLA Ops:
  7.2 22.9 %all-gather.2 = f32[16,96,32]{1,2,0:T(8,128)S(1)} all-gather(f32[1,96,32]{1,2,0:T(8,128)} %bitcast.68), channel_id=1, replica_groups=mesh['row'=16,'col'=16] {'row'}, dimensions={0}, use_global_device_ids=true | all-gather | bytes 208896 | tf_op jit(solution)/shard_map/all_gather | solution.py:59
  30.1 40.2 %all-gather.1 = f32[16,96,32]{1,2,0:T(8,128)S(1)} all-gather(f32[1,96,32]{1,2,0:T(8,128)} %bitcast.69), channel_id=1, replica_groups=mesh['row'=16,'col'=16] {'col'}, dimensions={0}, use_global_device_ids=true | all-gather | bytes 208896 | tf_op jit(solution)/shard_map/all_gather | solution.py:58
  70.3 0.8 fusion.54
  71.2 1.5 concatenate.27
  72.7 23.2 %all-gather = bf16[16,96,12]{1,2,0:T(8,128)(2,1)S(1)} all-gather(bf16[1,96,12]{1,2,0:T(8,128)(2,1)S(1)} %convert_bitcast_fusion.1), channel_id=1, replica_groups=mesh['row'=16,'col'=16] {'row'}, dimensions={0}, use_global_device_ids=true | all-gather | bytes 39168 | tf_op jit(solution)/shard_map/all_gather | solution.py:76
  96.8 0.7 fusion.56
  97.4 0.7 fusion.55
  98.1 2.8 fusion
  101.0 3.7 fusion.1
  104.7 1.9 fusion.10
  106.6 1.9 fusion.18
  108.5 1.8 fusion.12
  110.3 1.8 fusion.4
  112.1 1.9 fusion.14
  114.0 1.9 fusion.6
  116.0 1.9 fusion.16
  117.8 1.9 fusion.8
  119.7 3.9 fusion.2
  123.6 1.8 fusion.20
  125.4 1.9 fusion.22
  127.4 1.9 fusion.24
  129.3 1.9 fusion.26
  131.2 1.2 copy.16
  132.7 77.2 %reduce-scatter.7.cloned.1.call-done = f32[96,12]{1,0:T(8,128)} async-done(((f32[1536,12]{1,0:T(8,128)}), f32[96,12]{1,0:T(8,128)}) %reduce-scatter.7.cloned.1.call-update) | async-done | bytes 4624
  209.8 0.9 copy.17
  210.7 0.2 multiply_reduce_fusion.6
  210.9 75.8 %all-reduce = (f32[12]{0:T(128)S(1)}, f32[12]{0:T(128)S(1)}) all-reduce(f32[12]{0:T(128)S(1)} %get-tuple-element.6, f32[12]{0:T(128)S(1)} %get-tuple-element.5), channel_id=1, replica_groups=mesh['row'=16,'col'=16] {'row','col'}, use_global_device_ids=true, to_apply=%region_1.0 | all-reduce | flops 24 | bytes 192 | tf_op jit(solution)/shard_map/psum | solution.py:74
  286.7 0.2 multiply_reduce_fusion.5
  286.9 73.4 %psum.30 = f32[12]{0:T(128)S(1)} all-reduce(f32[12]{0:T(128)S(1)} %multiply_reduce_fusion.5), channel_id=1, replica_groups=mesh['row'=16,'col'=16] {'row','col'}, use_global_device_ids=true, to_apply=%region_10.0 | all-reduce | flops 12 | bytes 96 | tf_op jit(solution)/shard_map/psum | solution.py:92
  360.4 19.8 %all-gather.3 = bf16[16,96,12]{1,2,0:T(8,128)(2,1)S(1)} all-gather(bf16[1,96,12]{1,2,0:T(8,128)(2,1)S(1)} %convert_bitcast_fusion), channel_id=1, replica_groups=mesh['row'=16,'col'=16] {'row'}, dimensions={0}, use_global_device_ids=true | all-gather | bytes 39168 | tf_op jit(solution)/shard_map/all_gather | solution.py:76
  380.4 4.0 fusion.3
  384.3 1.9 fusion.5
  386.3 1.9 fusion.7
  388.2 1.9 fusion.9
  390.1 1.8 fusion.11
  391.9 1.9 fusion.13
  393.8 2.1 fusion.15
  396.0 1.9 fusion.17
  397.9 1.8 fusion.19
  399.6 1.9 fusion.21
  401.6 1.9 fusion.23
  403.5 1.9 fusion.25
  405.4 1.2 copy.18
  406.6 79.3 %reduce-scatter.9.cloned.1.call-done = f32[96,12]{1,0:T(8,128)} async-done(((f32[1536,12]{1,0:T(8,128)}), f32[96,12]{1,0:T(8,128)}) %reduce-scatter.9.cloned.1.call-update) | async-done | bytes 4624
  485.9 0.9 copy.19
  486.8 0.2 multiply_reduce_fusion.4
  487.0 75.8 %psum.31 = f32[12]{0:T(128)S(1)} all-reduce(f32[12]{0:T(128)S(1)} %multiply_reduce_fusion.4), channel_id=1, replica_groups=mesh['row'=16,'col'=16] {'row','col'}, use_global_device_ids=true, to_apply=%region_13.0 | all-reduce | flops 12 | bytes 96 | tf_op jit(solution)/shard_map/psum | solution.py:86
  562.8 0.7 multiply_subtract_fusion
  (40 shorter events, 1.4 us)
Async XLA Ops:
  7.2 89.6 %copy-start.7 = (f32[4]{0:T(128)S(1)}, f32[4]{0:T(128)}, u32[]{:S(2)}) copy-start(f32[4]{0:T(128)} %param.9) | copy-start | bytes 52
  7.2 90.3 %copy-start.5 = (f32[4]{0:T(128)S(1)}, f32[4]{0:T(128)}, u32[]{:S(2)}) copy-start(f32[4]{0:T(128)} %param.10) | copy-start | bytes 52
  7.2 202.6 %reduce-scatter.7.cloned.1.call-start = ((), (), s32[]{:S(2)}) async-start(), calls=%async_computation.2 | async-start | bytes 835584
  96.7 4.3 copy-start.4
  101.0 16.9 %copy-start.2 = (f32[512,1536]{1,0:T(8,128)}, f32[512,1536]{1,0:T(8,128)S(1)}, u32[]{:S(2)}) copy-start(f32[512,1536]{1,0:T(8,128)S(1)} %fusion) | copy-start | bytes 9437188
  123.6 5.7 copy-start
  129.2 3.2 copy-start.6
  132.4 353.5 %reduce-scatter.9.cloned.1.call-start = ((), (), s32[]{:S(2)}) async-start(), calls=%async_computation.3 | async-start | bytes 835584
  380.4 4.0 copy-start.3
  393.8 4.1 copy-start.1
Sparse Core Ops, SparseCore 0:
  132.6 77.2 reduce-scatter.6
  406.8 79.0 reduce-scatter.8
where the time goes:
time: 571 us; the launch traced here: 570 us
  blocking collectives  331 us (58%)
  waiting for transfers between devices  156 us (27%)
  matrix products  58 us (10%)
  between operations  14.2 us (2%)
  local copies, waits for them, and re-layouts  8.85 us (2%)
    unnamed x4, waiting for transfers between devices  156 us
    psum x1, blocking collectives, on_device(): res_norm = lax.psum(jnp.sum(residual * residual, axis=1), ('row', 'col'))  75.8 us
    psum x1, blocking collectives, on_device(): curvature = lax.psum(jnp.sum(direction * applied, axis=1), ('row', 'col'))  75.8 us
    psum x1, blocking collectives, on_device(): fresh_norm = lax.psum(jnp.sum(residual * residual, axis=1), ('row', 'col'))  73.4 us
    dot_general x24, matrix products, apply_tiles(): lax.dot_general(dir_cols[p * width:(p + 1) * width], tiles[p], (((1,), (1...  47.6 us
    all_gather x2, blocking collectives, on_device(): lax.all_gather(direction.astype(jnp.bfloat16), 'row', axis=1, tiled=True)  43 us
    all_gather x1, blocking collectives, on_device(): rows_x = lax.all_gather(points, 'col', axis=1, tiled=True)  40.2 us
    all_gather x1, blocking collectives, on_device(): cols_x = lax.all_gather(points, 'row', axis=1, tiled=True)  22.9 us
  transfers between devices with their start and end apart: 2, of which 2 were waited for; matrix products, arithmetic and copies ran while one was open for 0% of the time, Pallas kernels for 0%

commit v1 on v0

--- a/solution.py
+++ b/solution.py
@@ -71,7 +71,7 @@
     solution = jnp.zeros_like(right_side)
     residual = right_side
     direction = right_side
-    res_norm = lax.psum(jnp.sum(residual * residual, axis=1), ("row", "col"))
+    res_norm = jnp.sum(lax.all_gather(jnp.sum(residual * residual, axis=1), ("row", "col")), axis=0)
     for iteration in range(ITERATIONS):
         dir_cols = lax.all_gather(direction.astype(jnp.bfloat16), "row", axis=1, tiled=True)
         pieces = []

time: 571 us -> 572 us (level)
    unnamed x0 -> x1, blocking collectives: none -> 76 us
    psum x1 -> x0, blocking collectives: 75.8 us -> none  [on_device(): res_norm = lax.psum(jnp.sum(residual * residual, axis=1), ('row', 'col'))]
where the time goes in v1:
time: 572 us; the launch traced here: 571 us
  blocking collectives  331 us (58%)
  waiting for transfers between devices  156 us (27%)
  matrix products  58 us (10%)
  between operations  14.2 us (2%)
  local copies, waits for them, and re-layouts  9.27 us (2%)
    unnamed x4, waiting for transfers between devices  156 us
    unnamed x1, blocking collectives  76 us
    psum x1, blocking collectives, on_device(): curvature = lax.psum(jnp.sum(direction * applied, axis=1), ('row', 'col'))  75.8 us
    psum x1, blocking collectives, on_device(): fresh_norm = lax.psum(jnp.sum(residual * residual, axis=1), ('row', 'col'))  73.5 us
    dot_general x24, matrix products, apply_tiles(): lax.dot_general(dir_cols[p * width:(p + 1) * width], tiles[p], (((1,), (1...  47.6 us
    all_gather x2, blocking collectives, on_device(): lax.all_gather(direction.astype(jnp.bfloat16), 'row', axis=1, tiled=True)  43 us
    all_gather x1, blocking collectives, on_device(): rows_x = lax.all_gather(points, 'col', axis=1, tiled=True)  40.2 us
    all_gather x1, blocking collectives, on_device(): cols_x = lax.all_gather(points, 'row', axis=1, tiled=True)  22.9 us
  transfers between devices with their start and end apart: 2, of which 2 were waited for; matrix products, arithmetic and copies ran while one was open for 0% of the time, Pallas kernels for 0%

profile of v1, /device:TPU:1, one launch (start us, length us, event | category | flops | bytes accessed | tf_op | source)
XLA Modules:
  0.0 571.0 jit_solution(7420419001252950874)
XLA Ops:
  7.2 22.9 %all-gather.3 = f32[16,96,32]{1,2,0:T(8,128)S(1)} all-gather(f32[1,96,32]{1,2,0:T(8,128)} %bitcast.68), channel_id=1, replica_groups=mesh['row'=16,'col'=16] {'row'}, dimensions={0}, use_global_device_ids=true | all-gather | bytes 208896 | tf_op jit(solution)/shard_map/all_gather | solution.py:59
  30.1 40.2 %all-gather.2 = f32[16,96,32]{1,2,0:T(8,128)S(1)} all-gather(f32[1,96,32]{1,2,0:T(8,128)} %bitcast.69), channel_id=1, replica_groups=mesh['row'=16,'col'=16] {'col'}, dimensions={0}, use_global_device_ids=true | all-gather | bytes 208896 | tf_op jit(solution)/shard_map/all_gather | solution.py:58
  70.3 0.8 fusion.54
  71.2 1.5 concatenate.27
  72.7 23.2 %all-gather.1 = bf16[16,96,12]{1,2,0:T(8,128)(2,1)S(1)} all-gather(bf16[1,96,12]{1,2,0:T(8,128)(2,1)S(1)} %convert_bitcast_fusion.1), channel_id=1, replica_groups=mesh['row'=16,'col'=16] {'row'}, dimensions={0}, use_global_device_ids=true | all-gather | bytes 39168 | tf_op jit(solution)/shard_map/all_gather | solution.py:76
  96.8 0.7 fusion.56
  97.4 0.7 fusion.55
  98.1 2.8 fusion
  101.0 3.7 fusion.1
  104.7 1.9 fusion.10
  106.6 1.9 fusion.18
  108.5 1.8 fusion.12
  110.3 1.8 fusion.4
  112.1 1.9 fusion.14
  114.0 1.9 fusion.6
  116.0 1.9 fusion.16
  117.8 1.9 fusion.8
  119.7 3.9 fusion.2
  123.6 1.8 fusion.20
  125.4 1.9 fusion.22
  127.4 1.9 fusion.24
  129.3 1.9 fusion.26
  131.2 1.2 copy.16
  132.7 77.2 %reduce-scatter.7.cloned.1.call-done = f32[96,12]{1,0:T(8,128)} async-done(((f32[1536,12]{1,0:T(8,128)}), f32[96,12]{1,0:T(8,128)}) %reduce-scatter.7.cloned.1.call-update) | async-done | bytes 4624
  209.8 0.9 copy.17
  210.7 0.2 multiply_reduce_fusion.6
  210.9 0.3 dynamic-update-slice
  211.2 76.0 %all-reduce.1 = (f32[3072]{0:T(1024)S(1)}, f32[12]{0:T(128)S(1)}) all-reduce(f32[3072]{0:T(1024)S(1)} %dynamic-update-slice, f32[12]{0:T(128)S(1)} %get-tuple-element.5), channel_id=2, replica_groups=mesh['row'=16,'col'=16] {'row','col'}, use_global_device_ids=true, to_apply=%add | all-reduce | flops 3084 | bytes 24672
  287.5 73.5 %psum.22 = f32[12]{0:T(128)S(1)} all-reduce(f32[12]{0:T(128)S(1)} %multiply_reduce_fusion.5), channel_id=1, replica_groups=mesh['row'=16,'col'=16] {'row','col'}, use_global_device_ids=true, to_apply=%region_10.0 | all-reduce | flops 12 | bytes 96 | tf_op jit(solution)/shard_map/psum | solution.py:92
  361.1 19.8 %all-gather.4 = bf16[16,96,12]{1,2,0:T(8,128)(2,1)S(1)} all-gather(bf16[1,96,12]{1,2,0:T(8,128)(2,1)S(1)} %convert_bitcast_fusion), channel_id=1, replica_groups=mesh['row'=16,'col'=16] {'row'}, dimensions={0}, use_global_device_ids=true | all-gather | bytes 39168 | tf_op jit(solution)/shard_map/all_gather | solution.py:76
  381.1 4.0 fusion.3
  385.0 1.9 fusion.5
  387.0 1.9 fusion.7
  388.9 1.9 fusion.9
  390.8 1.8 fusion.11
  392.6 1.9 fusion.13
  394.5 2.1 fusion.15
  396.6 1.9 fusion.17
  398.6 1.8 fusion.19
  400.3 1.9 fusion.21
  402.3 1.9 fusion.23
  404.2 1.9 fusion.25
  406.1 1.2 copy.18
  407.3 79.3 %reduce-scatter.9.cloned.1.call-done = f32[96,12]{1,0:T(8,128)} async-done(((f32[1536,12]{1,0:T(8,128)}), f32[96,12]{1,0:T(8,128)}) %reduce-scatter.9.cloned.1.call-update) | async-done | bytes 4624
  486.6 0.9 copy.19
  487.4 0.2 multiply_reduce_fusion.4
  487.6 75.8 %psum.23 = f32[12]{0:T(128)S(1)} all-reduce(f32[12]{0:T(128)S(1)} %multiply_reduce_fusion.4), channel_id=1, replica_groups=mesh['row'=16,'col'=16] {'row','col'}, use_global_device_ids=true, to_apply=%region_13.0 | all-reduce | flops 12 | bytes 96 | tf_op jit(solution)/shard_map/psum | solution.py:86
  563.5 0.7 multiply_subtract_fusion
  (44 shorter events, 1.8 us)
Async XLA Ops:
  7.2 89.6 %copy-start.7 = (f32[4]{0:T(128)S(1)}, f32[4]{0:T(128)}, u32[]{:S(2)}) copy-start(f32[4]{0:T(128)} %param.9) | copy-start | bytes 52
  7.2 90.3 %copy-start.5 = (f32[4]{0:T(128)S(1)}, f32[4]{0:T(128)}, u32[]{:S(2)}) copy-start(f32[4]{0:T(128)} %param.10) | copy-start | bytes 52
  7.2 202.6 %reduce-scatter.7.cloned.1.call-start = ((), (), s32[]{:S(2)}) async-start(), calls=%async_computation.2 | async-start | bytes 835584
  96.7 4.3 copy-start.4
  101.0 16.9 %copy-start.2 = (f32[512,1536]{1,0:T(8,128)}, f32[512,1536]{1,0:T(8,128)S(1)}, u32[]{:S(2)}) copy-start(f32[512,1536]{1,0:T(8,128)S(1)} %fusion) | copy-start | bytes 9437188
  123.6 5.7 copy-start
  129.2 3.2 copy-start.6
  132.4 354.1 %reduce-scatter.9.cloned.1.call-start = ((), (), s32[]{:S(2)}) async-start(), calls=%async_computation.3 | async-start | bytes 835584
  381.0 4.0 copy-start.3
  394.5 4.1 copy-start.1
Sparse Core Ops, SparseCore 0:
  132.6 77.2 reduce-scatter.6
  407.5 79.0 reduce-scatter.8
